TPU v7x, 128 devices: a whole 4x4x4 slice. The times are simulated.
128 devices in a mesh: row: 8 (over x, core), col: 16 (over y, z).
Axes of the slice: x: 4, y: 4, z: 4, core: 2. Of those that a mesh axis runs over, the one named last changes fastest.
Arguments:
- valence: bfloat16 [2, 16, 32768], replicated, may hold values from -6 to 6
- conduction: bfloat16 [2, 128, 32768], replicated, may hold values from -6 to 6
- valence_energy: float32 [16], replicated, may hold values from -8 to -1
- conduction_energy: float32 [128], replicated, may hold values from 0.5 to 6
- band_pairs: int32 [1024, 2], P(('row', 'col')), may hold values from 0 to 127, as said below
- grid_index: int32 [16384], replicated, may hold values from 0 to 32767, as said below
Outputs:
- response: float32 [2, 16384, 16384], P(None, 'row', 'col')
Inputs may be any that keep to these rules, and one draw needn't show every extreme that they name: `band_pairs`: the rows are distinct combinations of a valence band below 16 and a conduction band below 128, half of all combinations. `grid_index`: the 16384 entries are distinct.
All inputs are finite; a program needn't handle non-finite values.
Results may differ from a plain program's by a relative error of at most 0.0039.
Values may be sent and summed in bfloat16 or wider, within the bound.
A program may use at most 192 MiB of HBM per device.

v0:
```python
import math
import jax
import jax.numpy as jnp
from jax import lax
from jax.sharding import PartitionSpec as P

N1 = 32
N2 = 32
N3 = 32
NVB = 16
NCB = 128


def tables(length):
    position = jnp.arange(length, dtype=jnp.int32)
    phase_angle = (position[:, None] * position[None, :] % length).astype(jnp.float32) * (
        2.0 * math.pi / length
    )
    return (jnp.cos(phase_angle), jnp.sin(phase_angle))


def plane_table():
    plane_size = N2 * N3
    position = jnp.arange(plane_size, dtype=jnp.int32)
    second = position // N3
    third = position % N3
    phase_index = (
        second[:, None] * second[None, :] % N2 * N3 + third[:, None] * third[None, :] % N3 * N2
    )
    phase_angle = (phase_index % plane_size).astype(jnp.float32) * (2.0 * math.pi / plane_size)
    cosine = jnp.cos(phase_angle)
    sine_table = jnp.sin(phase_angle)
    upper = jnp.concatenate([cosine, -sine_table], axis=1)
    lower = jnp.concatenate([sine_table, cosine], axis=1)
    return jnp.concatenate([upper, lower], axis=0)


def transform(rho_real, rho_imag):
    pair_count = rho_real.shape[0]
    plane_size = N2 * N3
    stacked = jnp.concatenate(
        [
            rho_real.reshape(pair_count, N1, plane_size),
            rho_imag.reshape(pair_count, N1, plane_size),
        ],
        axis=2,
    )
    plane = jnp.dot(
        stacked.reshape(pair_count * N1, 2 * plane_size),
        plane_table(),
        precision=lax.Precision.HIGHEST,
    )
    plane = plane.reshape(pair_count, N1, 2 * plane_size)
    cosine, sine_table = tables(N1)
    cos_part = jnp.einsum("kr,prx->pkx", cosine, plane, precision=lax.Precision.HIGHEST)
    sin_part = jnp.einsum("kr,prx->pkx", sine_table, plane, precision=lax.Precision.HIGHEST)
    out_real = cos_part[:, :, :plane_size] + sin_part[:, :, plane_size:]
    out_imag = cos_part[:, :, plane_size:] - sin_part[:, :, :plane_size]
    return (out_real.reshape(pair_count, -1), out_imag.reshape(pair_count, -1))


def pair_spectrum(valence, conduction, valence_energy, conduction_energy, band_pairs):
    valence_rows = jnp.take(valence, band_pairs[:, 0], axis=1).astype(jnp.float32)
    conduction_rows = jnp.take(conduction, band_pairs[:, 1], axis=1).astype(jnp.float32)
    rho_real = valence_rows[0] * conduction_rows[0] + valence_rows[1] * conduction_rows[1]
    rho_imag = valence_rows[0] * conduction_rows[1] - valence_rows[1] * conduction_rows[0]
    out_real, out_imag = transform(rho_real, rho_imag)
    normalize = 1.0 / math.sqrt(N1 * N2 * N3)
    spectrum = jnp.stack([out_real, out_imag]) * normalize
    valence_hot = (
        band_pairs[:, 0][:, None] == jnp.arange(valence_energy.shape[0], dtype=jnp.int32)[None, :]
    )
    conduction_hot = (
        band_pairs[:, 1][:, None]
        == jnp.arange(conduction_energy.shape[0], dtype=jnp.int32)[None, :]
    )
    energy_gap = jnp.sum(jnp.where(valence_hot, valence_energy[None, :], 0.0), axis=1) - jnp.sum(
        jnp.where(conduction_hot, conduction_energy[None, :], 0.0), axis=1
    )
    weights = 2.0 / (math.sqrt(NVB * NCB // 2) * energy_gap)
    return (spectrum, weights)


def contract(weighted_part, operand, left_dims, right_dims):
    full_left = (0,) + tuple((d + 1 for d in left_dims))
    full_right = (0,) + tuple((d + 1 for d in right_dims))
    real_part = lax.dot_general(
        weighted_part,
        operand,
        ((full_left, full_right), ((), ())),
        preferred_element_type=jnp.float32,
    )
    pair_dims = ((left_dims, right_dims), ((), ()))
    imag_part = lax.dot_general(
        weighted_part[0], operand[1], pair_dims, preferred_element_type=jnp.float32
    ) - lax.dot_general(weighted_part[1], operand[0], pair_dims, preferred_element_type=jnp.float32)
    return jnp.stack([real_part, imag_part])


def body(valence, conduction, valence_energy, conduction_energy, band_pairs, grid_index):
    spectrum, weights = pair_spectrum(
        valence, conduction, valence_energy, conduction_energy, band_pairs
    )
    row_count = lax.axis_size("row")
    column_count = lax.axis_size("col")
    selected = jnp.take(spectrum, grid_index, axis=2)
    weighted = (weights[None, :, None] * selected).astype(jnp.bfloat16)
    density = selected.astype(jnp.bfloat16)
    weighted_block = lax.all_to_all(weighted, "row", split_axis=2, concat_axis=1, tiled=True)
    density_block = lax.all_to_all(density, "col", split_axis=2, concat_axis=1, tiled=True)
    weighted_all = lax.all_gather(weighted_block, "col", axis=1, tiled=True)
    density_all = lax.all_gather(density_block, "row", axis=1, tiled=True)
    pair_count = density_all.shape[1]
    per_device = pair_count // (row_count * column_count)
    weighted_split = weighted_all.reshape(
        2, column_count, row_count, per_device, weighted_all.shape[2]
    )
    density_split = density_all.reshape(
        2, row_count, column_count, per_device, density_all.shape[2]
    )
    return contract(weighted_split, density_split, (0, 1, 2), (1, 0, 2))


def solution(mesh):
    return jax.shard_map(
        body,
        mesh=mesh,
        in_specs=(P(), P(), P(), P(), P(("row", "col"), None), P()),
        out_specs=P(None, "row", "col"),
        check_vma=False,
    )
```

profile of v0, /device:TPU:1, one launch (start us, length us, event | category | flops | bytes accessed | tf_op | source)
XLA Modules:
  0.0 724.0 jit_solution(14251131210681987142)
XLA Ops:
  6.5 0.0 copy-start
  6.5 0.0 all-gather.5.cloned.1.call-start
  6.5 0.8 fusion.55
  7.4 0.8 and_bitcast_fusion.1
  8.2 3.6 gather_fusion.1
  11.8 1.5 convert_bitcast_fusion.1
  13.3 0.0 copy-done
  13.3 3.5 gather_fusion
  16.9 0.0 copy-start.2
  16.9 0.2 convert_bitcast_fusion.2
  17.1 1.4 copy-done.2
  18.4 0.3 multiply_add_fusion
  18.8 0.6 copy.50
  19.4 0.6 copy.51
  20.0 23.7 %fusion.25 = (f32[1024,1024]{1,0:T(8,128)}, f32[1024,1024]{1,0:T(8,128)}, f32[1024,1024]{1,0:T(8,128)}) fusion(s32[1024]{0:T(1024)S(1)} %get-tuple-element.24, s32[1024]{0:T(1024)S(1)} %get-tuple-element.25), kind=kLoop, calls=%fused_computation.53 | loop fusion | flops 41943040 | bytes 12591104 | tf_op jit(solution)/shard_map/neg | solution.py:33
  43.7 22.3 %fusion = f32[8,32,2048]{2,1,0:T(8,128)} fusion(f32[1024,1024]{1,0:T(8,128)} %get-tuple-element.15, f32[1024,1024]{1,0:T(8,128)} %get-tuple-element.14, f32[1024,1024]{1,0:T(8,128)} %get-tuple-element.13, f32[8,32,1024]{2,1,0:T(8,128)S(1)} %bitcast.102, f32[8,32,1024]{2,1,0:T(8,128)S(1)} %bitcast.103), kind=kOutput, calls=%fused_computation.4 | convolution fusion | flops 12898009088 | bytes 16777216 | tf_op jit(solution)/shard_map/dot_general | solution.py:48
  66.0 0.0 copy-start.3
  66.0 0.0 copy-start.7
  66.0 3.8 convolution_bitcast_fusion.1
  69.9 0.0 copy-done.3
  69.9 2.1 convolution_bitcast_fusion.2
  72.0 0.0 copy-done.7
  72.0 1.4 slice_add_fusion
  73.4 2.4 stack_reshape.6
  75.8 1.2 stack_reshape.7
  77.0 1.7 maximum_multiply_fusion
  78.7 28.8 %copy.31 = f32[2,8,32768]{1,0,2:T(2,128)} copy(f32[2,8,32768]{2,1,0:T(8,128)S(1)} %maximum_multiply_fusion) | data formatting | bytes 4194304 | tf_op jit(solution)/shard_map/mul | solution.py:69
  107.5 251.9 %gather_fusion.2 = f32[16384,2,8]{2,1,0:T(2,128)} fusion(f32[2,8,32768]{1,0,2:T(2,128)} %copy.31, s32[16384]{0:T(1024)S(1)} %fusion.26), kind=kCustom, calls=%fused_computation.2 | custom fusion | bytes 2162688 | tf_op jit(solution)/shard_map/jit(_take)/gather | solution.py:106
  359.4 71.1 %fusion.59 = bf16[16384,2,8]{2,1,0:T(2,128)(2,1)} fusion(f32[16384,2,8]{2,1,0:T(2,128)} %gather_fusion.2, pred[16384]{0:T(1024)(128)(4,1)S(1)} %compare_and_fusion), kind=kLoop, calls=%fused_computation.113 | loop fusion | flops 262144 | bytes 1589248
  430.5 10.5 %reshape.154 = bf16[16,2,8192]{2,1,0:T(2,128)(2,1)S(1)} reshape(bf16[16384,2,8]{2,1,0:T(2,128)(2,1)} %fusion.59) | data formatting | bytes 1048576
  440.9 18.7 %all_to_all.36 = bf16[16,2,8192]{2,1,0:T(2,128)(2,1)S(1)} all-to-all(bf16[16,2,8192]{2,1,0:T(2,128)(2,1)S(1)} %reshape.154), channel_id=1, replica_groups=mesh['row'=8,'col'=16] {'col'}, dimensions={0} | all-to-all | bytes 1048576 | tf_op jit(solution)/shard_map/all_to_all | solution.py:110
  459.6 10.9 %reshape.155 = bf16[16384,2,8]{2,1,0:T(2,128)(2,1)} reshape(bf16[16,2,8192]{2,1,0:T(2,128)(2,1)S(1)} %all_to_all.36) | data formatting | bytes 1048576
  470.6 0.0 copy-start.8
  470.6 0.0 copy-start.9
  470.6 19.3 %copy.33 = bf16[2,16,8,1024]{3,2,1,0:T(8,128)(2,1)} copy(bf16[2,16,8,1024]{2,0,3,1:T(2,128)(2,1)} %bitcast.90) | data formatting | bytes 1048576 | tf_op jit(solution)/shard_map/all_to_all | solution.py:110
  489.8 0.0 all-gather.5.cloned.1.call-update
  489.8 0.0 all-gather.3.cloned.1.call-start
  489.9 0.0 copy-done.8
  489.9 0.2 select_reduce_fusion
  490.1 0.0 copy-done.9
  490.1 0.2 select_reduce_fusion.1
  490.3 59.2 %fusion.60 = bf16[16384,2,8]{2,1,0:T(2,128)(2,1)} fusion(f32[16384,2,8]{2,1,0:T(2,128)} %gather_fusion.2, pred[16384]{0:T(1024)(128)(4,1)S(1)} %compare_and_fusion, f32[8]{0:T(128)S(1)} %multiply_divide_fusion), kind=kLoop, calls=%fused_computation.114 | loop fusion | flops 786432 | bytes 1589280
  549.4 10.4 %reshape.152 = bf16[8,2,16384]{2,1,0:T(2,128)(2,1)S(1)} reshape(bf16[16384,2,8]{2,1,0:T(2,128)(2,1)} %fusion.60) | data formatting | bytes 1048576
  559.9 15.6 %all_to_all.37 = bf16[8,2,16384]{2,1,0:T(2,128)(2,1)S(1)} all-to-all(bf16[8,2,16384]{2,1,0:T(2,128)(2,1)S(1)} %reshape.152), channel_id=1, replica_groups=mesh['row'=8,'col'=16] {'row'}, dimensions={0} | all-to-all | bytes 1048576 | tf_op jit(solution)/shard_map/all_to_all | solution.py:109
  575.5 10.9 %reshape.153 = bf16[16384,2,8]{2,1,0:T(2,128)(2,1)} reshape(bf16[8,2,16384]{2,1,0:T(2,128)(2,1)S(1)} %all_to_all.37) | data formatting | bytes 1048576
  586.3 19.2 %copy.32 = bf16[2,8,8,2048]{3,2,1,0:T(8,128)(2,1)} copy(bf16[2,8,8,2048]{2,0,3,1:T(2,128)(2,1)} %bitcast.91) | data formatting | bytes 1048576 | tf_op jit(solution)/shard_map/all_to_all | solution.py:109
  605.5 0.0 all-gather.3.cloned.1.call-update
  605.5 0.0 all-gather.5.cloned.1.call-done
  605.6 4.7 fusion.58
  610.2 62.7 %all-gather.3.cloned.1.call-done = bf16[2,1024,2048]{2,1,0:T(8,128)(2,1)} async-done(((bf16[2,64,2048]{2,1,0:T(8,128)(2,1)}), bf16[2,1024,2048]{2,1,0:T(8,128)(2,1)}) %all-gather.3.cloned.1.call-update) | async-done | bytes 8388624 | tf_op jit(solution)/shard_map/all_gather | solution.py:111
  672.9 14.5 %convolution_bitcast_fusion = f32[1,2048,1024]{2,1,0:T(8,128)} fusion(bf16[2,16,8,8,2048]{4,3,2,1,0:T(8,128)(2,1)} %bitcast.92, bf16[2,8,16,8,1024]{4,3,2,1,0:T(8,128)(2,1)} %bitcast.93), kind=kOutput, calls=%fused_computation.31 | convolution fusion | flops 8589934592 | bytes 20971520 | tf_op jit(solution)/shard_map/dot_general | solution.py:87
  687.4 0.0 copy-start.6
  687.4 5.4 fusion.57
  692.8 0.0 copy-done.6
  692.8 0.0 copy-start.4
  692.8 0.0 copy-start.5
  692.8 6.9 fusion.21
  699.7 0.0 copy-done.4
  699.7 0.0 copy-done.5
  699.8 7.4 %fusion.8 = f32[1,2048,1024]{2,1,0:T(8,128)S(1)} fusion(f32[2048,1024,1,1]{1,0,3,2:T(8,128)} %fusion.21, bf16[16,8,8,2048]{3,2,1,0:T(8,128)(2,1)S(1)} %bitcast.96, bf16[8,16,8,1024]{3,2,1,0:T(8,128)(2,1)S(1)} %bitcast.100), kind=kOutput, calls=%fused_computation.16 | convolution fusion | flops 4297064448 | bytes 23068672 | tf_op jit(solution)/shard_map/dot_general | solution.py:96
  707.1 0.0 copy-start.1
  707.2 10.0 %pad_maximum_fusion = f32[2,2048,1024]{2,1,0:T(8,128)} fusion(f32[1,2048,1024]{2,1,0:T(8,128)S(1)} %fusion.8, f32[1,2048,1024]{2,1,0:T(8,128)} %convolution_bitcast_fusion), kind=kLoop, calls=%fused_computation.11 | loop fusion | flops 4194304 | bytes 33554432 | tf_op jit(solution)/shard_map/stack | solution.py:97
  717.2 0.0 copy-done.1
  (5 shorter events, 0.1 us)
Async XLA Ops:
  6.5 6.8 copy-start
  6.5 599.0 %all-gather.5.cloned.1.call-start = ((), (), s32[]{:S(2)}) async-start(), calls=%async_computation.3 | async-start | bytes 4718592 | tf_op jit(solution)/shard_map/all_gather | solution.py:112
  16.9 1.6 copy-start.2
  66.0 3.8 copy-start.3
  66.0 6.0 copy-start.7
  470.6 19.3 %copy-start.8 = (f32[128]{0:T(128)S(1)}, f32[128]{0:T(128)}, u32[]{:S(2)}) copy-start(f32[128]{0:T(128)} %param.9) | copy-start | bytes 1540
  470.6 19.5 %copy-start.9 = (f32[16]{0:T(128)S(1)}, f32[16]{0:T(128)}, u32[]{:S(2)}) copy-start(f32[16]{0:T(128)} %param.8) | copy-start | bytes 196
  489.8 183.1 %all-gather.3.cloned.1.call-start = ((), (), s32[]{:S(2)}) async-start(), calls=%async_computation.2 | async-start | bytes 8912896 | tf_op jit(solution)/shard_map/all_gather | solution.py:111
  687.4 5.4 copy-start.6
  692.8 7.0 copy-start.4
  692.8 7.0 copy-start.5
  707.1 10.0 %copy-start.1 = (bf16[2,16,32768]{2,1,0:T(8,128)(2,1)S(1)}, bf16[2,16,32768]{2,1,0:T(8,128)(2,1)}, u32[]{:S(2)}) copy-start(bf16[2,16,32768]{2,1,0:T(8,128)(2,1)} %param.6) | copy-start | bytes 6291460
Sparse Core Ops, SparseCore 0:
  490.0 31.7 all-gather.4
  605.7 67.1 all-gather.2
where the time goes:
time: 734 us; the launch traced here: 724 us
  local copies, waits for them, and re-layouts  385 us (52%)
  other arithmetic  171 us (23%)
  waiting for transfers between devices  62.7 us (9%)
  matrix products  57 us (8%)
  blocking collectives  34.3 us (5%)
  between operations  13.6 us (2%)
    gather x1, local copies, waits for them, and re-layouts, body(): selected = jnp.take(spectrum, grid_index, axis=2)  252 us
    unnamed x2, other arithmetic  130 us
    all_gather x1, waiting for transfers between devices, body(): weighted_all = lax.all_gather(weighted_block, 'col', axis=1, tiled=True)  62.7 us
    unnamed x26, local copies, waits for them, and re-layouts  45.3 us
    mul x1, local copies, waits for them, and re-layouts, pair_spectrum(): spectrum = jnp.stack([out_real, out_imag]) * normalize  28.8 us
    neg x1, other arithmetic, plane_table(): upper = jnp.concatenate([cosine, -sine_table], axis=1)  23.7 us
    dot_general x1, matrix products, transform(): jnp.dot(stacked.reshape(pair_count * N1, 2 * plane_size), plane_table(),...  22.3 us
    all_to_all x1, local copies, waits for them, and re-layouts, body(): lax.all_to_all(density, 'col', split_axis=2, concat_axis=1, tiled=True)  19.3 us
  transfers between devices with their start and end apart: 2, of which 1 were waited for; matrix products, arithmetic and copies ran while one was open for 14% of the time, Pallas kernels for 0%

commit v1 on v0

--- a/solution.py
+++ b/solution.py
@@ -108,7 +108,12 @@
     density = selected.astype(jnp.bfloat16)
     weighted_block = lax.all_to_all(weighted, "row", split_axis=2, concat_axis=1, tiled=True)
     density_block = lax.all_to_all(density, "col", split_axis=2, concat_axis=1, tiled=True)
-    weighted_all = lax.all_gather(weighted_block, "col", axis=1, tiled=True)
+    ring = [weighted_block]
+    for hop in range(15):
+        ring.append(lax.ppermute(ring[-1], "col", [(dev, (dev + 1) % 16) for dev in range(16)]))
+    weighted_all = jnp.roll(
+        jnp.concatenate(ring[::-1], axis=1), (lax.axis_index("col") + 1) * ring[0].shape[1], axis=1
+    )
     density_all = lax.all_gather(density_block, "row", axis=1, tiled=True)
     pair_count = density_all.shape[1]
     per_device = pair_count // (row_count * column_count)

time: 734 us -> 896 us (1.22)
  the two profiles are of different devices: /device:TPU:1 before, /device:TPU:0 now
where the time goes in v1:
time: 896 us; the launch traced here: 886 us
  local copies, waits for them, and re-layouts  433 us (48%)
  waiting for transfers between devices  204 us (23%)
  other arithmetic  159 us (18%)
  matrix products  60.4 us (7%)
  starting transfers between devices  16 us (2%)
  between operations  13.9 us (2%)
    gather x1, local copies, waits for them, and re-layouts, body(): selected = jnp.take(spectrum, grid_index, axis=2)  252 us
    ppermute x15, waiting for transfers between devices, body(): lax.ppermute(ring[-1], 'col', [(dev, (dev + 1) % 16) for dev in range(16)])  204 us
    unnamed x2, other arithmetic  118 us
    unnamed x87, local copies, waits for them, and re-layouts  82 us
    mul x1, local copies, waits for them, and re-layouts, pair_spectrum(): spectrum = jnp.stack([out_real, out_imag]) * normalize  28.8 us
    neg x1, other arithmetic, plane_table(): upper = jnp.concatenate([cosine, -sine_table], axis=1)  23.9 us
    dot_general x1, matrix products, transform(): jnp.dot(stacked.reshape(pair_count * N1, 2 * plane_size), plane_table(),...  22.3 us
    all_to_all x1, local copies, waits for them, and re-layouts, body(): lax.all_to_all(density, 'col', split_axis=2, concat_axis=1, tiled=True)  19.2 us
  transfers between devices with their start and end apart: 18, of which 14 were waited for; matrix products, arithmetic and copies ran while one was open for 15% of the time, Pallas kernels for 0%

profile of v1, /device:TPU:0, one launch (start us, length us, event | category | flops | bytes accessed | tf_op | source)
XLA Modules:
  0.0 885.6 jit_solution(4470813232845200093)
XLA Ops:
  6.5 0.9 and_bitcast_fusion.1
  8.2 0.9 compare_and_fusion
  9.0 0.9 fusion.26
  9.9 3.6 gather_fusion.1
  13.5 1.5 convert_bitcast_fusion.1
  15.0 3.5 gather_fusion
  18.8 1.8 multiply_add_fusion
  21.8 23.9 %fusion.25 = (f32[1024,1024]{1,0:T(8,128)}, f32[1024,1024]{1,0:T(8,128)}, f32[1024,1024]{1,0:T(8,128)}) fusion(s32[1024]{0:T(1024)S(1)} %get-tuple-element.22, s32[1024]{0:T(1024)S(1)} %get-tuple-element.23), kind=kLoop, calls=%fused_computation.53 | loop fusion | flops 41943040 | bytes 12591104 | tf_op jit(solution)/shard_map/neg | solution.py:33
  45.7 22.3 %fusion = f32[8,32,2048]{2,1,0:T(8,128)} fusion(f32[1024,1024]{1,0:T(8,128)} %get-tuple-element.15, f32[1024,1024]{1,0:T(8,128)} %get-tuple-element.14, f32[1024,1024]{1,0:T(8,128)} %get-tuple-element.13, f32[8,32,1024]{2,1,0:T(8,128)S(1)} %bitcast.105, f32[8,32,1024]{2,1,0:T(8,128)S(1)} %bitcast.104), kind=kOutput, calls=%fused_computation.4 | convolution fusion | flops 12898009088 | bytes 16777216 | tf_op jit(solution)/shard_map/dot_general | solution.py:48
  67.9 3.7 convolution_bitcast_fusion.1
  71.6 3.7 convolution_bitcast_fusion.2
  75.3 1.4 slice_add_fusion
  76.7 2.4 stack_reshape.6
  79.1 1.2 stack_reshape.7
  80.2 1.7 maximum_multiply_fusion
  82.0 28.8 %copy.31 = f32[2,8,32768]{1,0,2:T(2,128)} copy(f32[2,8,32768]{2,1,0:T(8,128)S(1)} %maximum_multiply_fusion) | data formatting | bytes 4194304 | tf_op jit(solution)/shard_map/mul | solution.py:69
  111.2 251.9 %gather_fusion.2 = f32[16384,2,8]{2,1,0:T(2,128)} fusion(f32[2,8,32768]{1,0,2:T(2,128)} %copy.31, s32[16384]{0:T(1024)S(1)} %fusion.26), kind=kCustom, calls=%fused_computation.2 | custom fusion | bytes 2162688 | tf_op jit(solution)/shard_map/jit(_take)/gather | solution.py:106
  363.0 59.3 %fusion.59 = bf16[16384,2,8]{2,1,0:T(2,128)(2,1)} fusion(f32[16384,2,8]{2,1,0:T(2,128)} %gather_fusion.2, pred[16384]{0:T(1024)(128)(4,1)S(1)} %compare_and_fusion, f32[8]{0:T(128)S(1)} %multiply_divide_fusion), kind=kLoop, calls=%fused_computation.148 | loop fusion | flops 786432 | bytes 1589280
  422.3 11.2 %reshape.152 = bf16[8,2,16384]{2,1,0:T(2,128)(2,1)} reshape(bf16[16384,2,8]{2,1,0:T(2,128)(2,1)} %fusion.59) | data formatting | bytes 1048576
  433.5 4.4 all-to-all-start
  437.9 59.1 %fusion.58 = bf16[16384,2,8]{2,1,0:T(2,128)(2,1)} fusion(f32[16384,2,8]{2,1,0:T(2,128)} %gather_fusion.2, pred[16384]{0:T(1024)(128)(4,1)S(1)} %compare_and_fusion), kind=kLoop, calls=%fused_computation.147 | loop fusion | flops 262144 | bytes 1589248
  497.0 11.2 %reshape.154 = bf16[16,2,8192]{2,1,0:T(2,128)(2,1)} reshape(bf16[16384,2,8]{2,1,0:T(2,128)(2,1)} %fusion.58) | data formatting | bytes 1048576
  508.2 8.0 all-to-all-start.1
  516.3 10.9 %reshape.153 = bf16[16384,2,8]{2,1,0:T(2,128)(2,1)} reshape(bf16[8,2,16384]{2,1,0:T(2,128)(2,1)S(1)} %all-to-all-done) | data formatting | bytes 1048576
  527.2 17.7 %copy.32 = bf16[2,8,8,2048]{3,2,1,0:T(8,128)(2,1)S(1)} copy(bf16[2,8,8,2048]{2,0,3,1:T(2,128)(2,1)} %bitcast.92) | data formatting | bytes 1048576 | tf_op jit(solution)/shard_map/all_to_all | solution.py:109
  544.8 2.0 collective-permute-start
  546.8 10.9 %reshape.155 = bf16[16384,2,8]{2,1,0:T(2,128)(2,1)} reshape(bf16[16,2,8192]{2,1,0:T(2,128)(2,1)S(1)} %all-to-all-done.1) | data formatting | bytes 1048576
  557.7 19.2 %copy.33 = bf16[2,16,8,1024]{3,2,1,0:T(8,128)(2,1)} copy(bf16[2,16,8,1024]{2,0,3,1:T(2,128)(2,1)} %bitcast.93) | data formatting | bytes 1048576 | tf_op jit(solution)/shard_map/all_to_all | solution.py:110
  576.9 1.5 collective-permute-start.1
  578.5 15.4 %collective-permute-done.1 = bf16[2,64,2048]{2,1,0:T(8,128)(2,1)S(1)} collective-permute-done((bf16[2,64,2048]{2,1,0:T(8,128)(2,1)S(1)}, bf16[2,64,2048]{2,1,0:T(8,128)(2,1)S(1)}, u32[]{:S(2)}, u32[]{:S(2)}) %collective-permute-start.1) | collective-permute-done | bytes 524320 | tf_op jit(solution)/shard_map/ppermute | solution.py:113
  593.8 15.9 %collective-permute-done.2 = bf16[2,64,2048]{2,1,0:T(8,128)(2,1)S(1)} collective-permute-done((bf16[2,64,2048]{2,1,0:T(8,128)(2,1)S(1)}, bf16[2,64,2048]{2,1,0:T(8,128)(2,1)S(1)}, u32[]{:S(2)}, u32[]{:S(2)}) %collective-permute-start.2) | collective-permute-done | bytes 524320 | tf_op jit(solution)/shard_map/ppermute | solution.py:113
  609.7 15.0 %collective-permute-done.3 = bf16[2,64,2048]{2,1,0:T(8,128)(2,1)S(1)} collective-permute-done((bf16[2,64,2048]{2,1,0:T(8,128)(2,1)S(1)}, bf16[2,64,2048]{2,1,0:T(8,128)(2,1)S(1)}, u32[]{:S(2)}, u32[]{:S(2)}) %collective-permute-start.3) | collective-permute-done | bytes 524320 | tf_op jit(solution)/shard_map/ppermute | solution.py:113
  624.7 14.1 %collective-permute-done.4 = bf16[2,64,2048]{2,1,0:T(8,128)(2,1)S(1)} collective-permute-done((bf16[2,64,2048]{2,1,0:T(8,128)(2,1)S(1)}, bf16[2,64,2048]{2,1,0:T(8,128)(2,1)S(1)}, u32[]{:S(2)}, u32[]{:S(2)}) %collective-permute-start.4) | collective-permute-done | bytes 524320 | tf_op jit(solution)/shard_map/ppermute | solution.py:113
  638.8 13.2 %collective-permute-done.5 = bf16[2,64,2048]{2,1,0:T(8,128)(2,1)S(1)} collective-permute-done((bf16[2,64,2048]{2,1,0:T(8,128)(2,1)S(1)}, bf16[2,64,2048]{2,1,0:T(8,128)(2,1)S(1)}, u32[]{:S(2)}, u32[]{:S(2)}) %collective-permute-start.5) | collective-permute-done | bytes 524320 | tf_op jit(solution)/shard_map/ppermute | solution.py:113
  652.8 12.5 %collective-permute-done.6 = bf16[2,64,2048]{2,1,0:T(8,128)(2,1)S(1)} collective-permute-done((bf16[2,64,2048]{2,1,0:T(8,128)(2,1)S(1)}, bf16[2,64,2048]{2,1,0:T(8,128)(2,1)S(1)}, u32[]{:S(2)}, u32[]{:S(2)}) %collective-permute-start.6) | collective-permute-done | bytes 524320 | tf_op jit(solution)/shard_map/ppermute | solution.py:113
  666.1 12.9 %collective-permute-done.7 = bf16[2,64,2048]{2,1,0:T(8,128)(2,1)S(1)} collective-permute-done((bf16[2,64,2048]{2,1,0:T(8,128)(2,1)S(1)}, bf16[2,64,2048]{2,1,0:T(8,128)(2,1)S(1)}, u32[]{:S(2)}, u32[]{:S(2)}) %collective-permute-start.7) | collective-permute-done | bytes 524320 | tf_op jit(solution)/shard_map/ppermute | solution.py:113
  679.8 14.0 %collective-permute-done.8 = bf16[2,64,2048]{2,1,0:T(8,128)(2,1)S(1)} collective-permute-done((bf16[2,64,2048]{2,1,0:T(8,128)(2,1)S(1)}, bf16[2,64,2048]{2,1,0:T(8,128)(2,1)S(1)}, u32[]{:S(2)}, u32[]{:S(2)}) %collective-permute-start.8) | collective-permute-done | bytes 524320 | tf_op jit(solution)/shard_map/ppermute | solution.py:113
  694.7 15.1 %collective-permute-done.9 = bf16[2,64,2048]{2,1,0:T(8,128)(2,1)S(1)} collective-permute-done((bf16[2,64,2048]{2,1,0:T(8,128)(2,1)S(1)}, bf16[2,64,2048]{2,1,0:T(8,128)(2,1)S(1)}, u32[]{:S(2)}, u32[]{:S(2)}) %collective-permute-start.9) | collective-permute-done | bytes 524320 | tf_op jit(solution)/shard_map/ppermute | solution.py:113
  710.5 16.2 %collective-permute-done.10 = bf16[2,64,2048]{2,1,0:T(8,128)(2,1)S(1)} collective-permute-done((bf16[2,64,2048]{2,1,0:T(8,128)(2,1)S(1)}, bf16[2,64,2048]{2,1,0:T(8,128)(2,1)S(1)}, u32[]{:S(2)}, u32[]{:S(2)}) %collective-permute-start.10) | collective-permute-done | bytes 524320 | tf_op jit(solution)/shard_map/ppermute | solution.py:113
  727.5 17.3 %collective-permute-done.11 = bf16[2,64,2048]{2,1,0:T(8,128)(2,1)S(1)} collective-permute-done((bf16[2,64,2048]{2,1,0:T(8,128)(2,1)S(1)}, bf16[2,64,2048]{2,1,0:T(8,128)(2,1)S(1)}, u32[]{:S(2)}, u32[]{:S(2)}) %collective-permute-start.11) | collective-permute-done | bytes 524320 | tf_op jit(solution)/shard_map/ppermute | solution.py:113
  745.7 17.7 %collective-permute-done.12 = bf16[2,64,2048]{2,1,0:T(8,128)(2,1)S(1)} collective-permute-done((bf16[2,64,2048]{2,1,0:T(8,128)(2,1)S(1)}, bf16[2,64,2048]{2,1,0:T(8,128)(2,1)S(1)}, u32[]{:S(2)}, u32[]{:S(2)}) %collective-permute-start.12) | collective-permute-done | bytes 524320 | tf_op jit(solution)/shard_map/ppermute | solution.py:113
  764.2 16.5 %collective-permute-done.13 = bf16[2,64,2048]{2,1,0:T(8,128)(2,1)} collective-permute-done((bf16[2,64,2048]{2,1,0:T(8,128)(2,1)S(1)}, bf16[2,64,2048]{2,1,0:T(8,128)(2,1)}, u32[]{:S(2)}, u32[]{:S(2)}) %collective-permute-start.13) | collective-permute-done | bytes 524320 | tf_op jit(solution)/shard_map/ppermute | solution.py:113
  780.8 4.9 fusion.57
  785.6 7.9 collective-permute-done.14
  793.5 1.9 constant_dynamic-update-slice_fusion.31
  795.4 1.9 constant_dynamic-update-slice_fusion.30
  797.3 0.8 constant_dynamic-update-slice_fusion.29
  798.1 0.8 constant_dynamic-update-slice_fusion.28
  805.7 0.8 constant_dynamic-update-slice_fusion.19
  806.5 0.8 constant_dynamic-update-slice_fusion.18
  807.4 0.8 constant_dynamic-update-slice_fusion.17
  808.2 0.8 constant_dynamic-update-slice_fusion.16
  809.1 1.9 constant_dynamic-update-slice_fusion.15
  810.9 1.9 constant_dynamic-update-slice_fusion.14
  821.2 0.8 constant_dynamic-update-slice_fusion.3
  822.0 0.8 constant_dynamic-update-slice_fusion.2
  822.9 0.8 constant_dynamic-update-slice_fusion.1
  823.7 0.8 constant_dynamic-update-slice_fusion
  824.6 8.3 constant_dynamic-slice_fusion.2
  832.9 8.5 constant_dynamic-slice_fusion
  841.4 13.2 %convolution_bitcast_fusion = f32[1,2048,1024]{2,1,0:T(8,128)} fusion(bf16[2,16,8,8,2048]{4,3,2,1,0:T(8,128)(2,1)S(1)} %bitcast.94, bf16[2,8,16,8,1024]{4,3,2,1,0:T(8,128)(2,1)} %bitcast.96), kind=kOutput, calls=%fused_computation.31 | convolution fusion | flops 8589934592 | bytes 20971520 | tf_op jit(solution)/shard_map/dot_general | solution.py:87
  854.6 6.9 fusion.21
  861.5 10.8 %fusion.8 = f32[1,2048,1024]{2,1,0:T(8,128)S(1)} fusion(f32[2048,1024,1,1]{1,0,3,2:T(8,128)} %fusion.21, bf16[16,8,8,2048]{3,2,1,0:T(8,128)(2,1)} %bitcast.99, bf16[8,16,8,1024]{3,2,1,0:T(8,128)(2,1)S(1)} %bitcast.102), kind=kOutput, calls=%fused_computation.16 | convolution fusion | flops 4297064448 | bytes 23068672 | tf_op jit(solution)/shard_map/dot_general | solution.py:96
  872.2 6.2 pad_maximum_fusion
  (96 shorter events, 24.3 us)
Async XLA Ops:
  6.5 8.5 copy-start
  82.0 28.8 %copy-start.23 = (f32[128]{0:T(128)S(1)}, f32[128]{0:T(128)}, u32[]{:S(2)}) copy-start(f32[128]{0:T(128)} %param.9) | copy-start | bytes 1540
  82.0 29.0 %copy-start.24 = (f32[16]{0:T(128)S(1)}, f32[16]{0:T(128)}, u32[]{:S(2)}) copy-start(f32[16]{0:T(128)} %param.8) | copy-start | bytes 196
  433.5 74.7 %all-to-all-start = ((bf16[8,2,16384]{2,1,0:T(2,128)(2,1)}), bf16[8,2,16384]{2,1,0:T(2,128)(2,1)S(1)}, u32[]{:S(2)}, u32[]{:S(2)}) async-start(bf16[8,2,16384]{2,1,0:T(2,128)(2,1)} %reshape.152), calls=%async_computation | async-start | bytes 1048576 | tf_op jit(solution)/shard_map/all_to_all | solution.py:109
  508.2 38.6 %all-to-all-start.1 = ((bf16[16,2,8192]{2,1,0:T(2,128)(2,1)}), bf16[16,2,8192]{2,1,0:T(2,128)(2,1)S(1)}, u32[]{:S(2)}, u32[]{:S(2)}) async-start(bf16[16,2,8192]{2,1,0:T(2,128)(2,1)} %reshape.154), calls=%async_computation.1 | async-start | bytes 1048576 | tf_op jit(solution)/shard_map/all_to_all | solution.py:110
  516.2 264.5 %all-gather.2.cloned.1.call-start = ((), (), s32[]{:S(2)}) async-start(), calls=%async_computation.2 | async-start | bytes 4718592 | tf_op jit(solution)/shard_map/all_gather | solution.py:117
  544.8 32.1 %collective-permute-start = (bf16[2,64,2048]{2,1,0:T(8,128)(2,1)S(1)}, bf16[2,64,2048]{2,1,0:T(8,128)(2,1)S(1)}, u32[]{:S(2)}, u32[]{:S(2)}) collective-permute-start(bf16[2,64,2048]{2,1,0:T(8,128)(2,1)S(1)} %bitcast.95), channel_id=1, source_target_pairs={{0,1},{1,2},{2,3},{3,4},{4,5},{5,6},{6,7},{7,8},{8,9},{9,10},{10,1... | collective-permute-start | bytes 1572872 | tf_op jit(solution)/shard_map/ppermute | solution.py:113
  576.9 16.9 %collective-permute-start.1 = (bf16[2,64,2048]{2,1,0:T(8,128)(2,1)S(1)}, bf16[2,64,2048]{2,1,0:T(8,128)(2,1)S(1)}, u32[]{:S(2)}, u32[]{:S(2)}) collective-permute-start(bf16[2,64,2048]{2,1,0:T(8,128)(2,1)S(1)} %collective-permute-done), channel_id=1, source_target_pairs={{0,1},{1,2},{2,3},{3,4},{4,5},{5,6},{6,7},{7,8},{8,9},{9,10},{10,1... | collective-permute-start | bytes 1572872 | tf_op jit(solution)/shard_map/ppermute | solution.py:113
  593.8 15.9 %collective-permute-start.2 = (bf16[2,64,2048]{2,1,0:T(8,128)(2,1)S(1)}, bf16[2,64,2048]{2,1,0:T(8,128)(2,1)S(1)}, u32[]{:S(2)}, u32[]{:S(2)}) collective-permute-start(bf16[2,64,2048]{2,1,0:T(8,128)(2,1)S(1)} %collective-permute-done.1), channel_id=1, source_target_pairs={{0,1},{1,2},{2,3},{3,4},{4,5},{5,6},{6,7},{7,8},{8,9},{9,10},{10,1... | collective-permute-start | bytes 1572872 | tf_op jit(solution)/shard_map/ppermute | solution.py:113
  609.7 15.0 %collective-permute-start.3 = (bf16[2,64,2048]{2,1,0:T(8,128)(2,1)S(1)}, bf16[2,64,2048]{2,1,0:T(8,128)(2,1)S(1)}, u32[]{:S(2)}, u32[]{:S(2)}) collective-permute-start(bf16[2,64,2048]{2,1,0:T(8,128)(2,1)S(1)} %collective-permute-done.2), channel_id=1, source_target_pairs={{0,1},{1,2},{2,3},{3,4},{4,5},{5,6},{6,7},{7,8},{8,9},{9,10},{10,1... | collective-permute-start | bytes 1572872 | tf_op jit(solution)/shard_map/ppermute | solution.py:113
  624.7 14.1 %collective-permute-start.4 = (bf16[2,64,2048]{2,1,0:T(8,128)(2,1)S(1)}, bf16[2,64,2048]{2,1,0:T(8,128)(2,1)S(1)}, u32[]{:S(2)}, u32[]{:S(2)}) collective-permute-start(bf16[2,64,2048]{2,1,0:T(8,128)(2,1)S(1)} %collective-permute-done.3), channel_id=1, source_target_pairs={{0,1},{1,2},{2,3},{3,4},{4,5},{5,6},{6,7},{7,8},{8,9},{9,10},{10,1... | collective-permute-start | bytes 1572872 | tf_op jit(solution)/shard_map/ppermute | solution.py:113
  638.8 13.2 %collective-permute-start.5 = (bf16[2,64,2048]{2,1,0:T(8,128)(2,1)S(1)}, bf16[2,64,2048]{2,1,0:T(8,128)(2,1)S(1)}, u32[]{:S(2)}, u32[]{:S(2)}) collective-permute-start(bf16[2,64,2048]{2,1,0:T(8,128)(2,1)S(1)} %collective-permute-done.4), channel_id=1, source_target_pairs={{0,1},{1,2},{2,3},{3,4},{4,5},{5,6},{6,7},{7,8},{8,9},{9,10},{10,1... | collective-permute-start | bytes 1572872 | tf_op jit(solution)/shard_map/ppermute | solution.py:113
  652.0 0.8 copy-start.5
  652.8 12.5 %collective-permute-start.6 = (bf16[2,64,2048]{2,1,0:T(8,128)(2,1)S(1)}, bf16[2,64,2048]{2,1,0:T(8,128)(2,1)S(1)}, u32[]{:S(2)}, u32[]{:S(2)}) collective-permute-start(bf16[2,64,2048]{2,1,0:T(8,128)(2,1)S(1)} %collective-permute-done.5), channel_id=1, source_target_pairs={{0,1},{1,2},{2,3},{3,4},{4,5},{5,6},{6,7},{7,8},{8,9},{9,10},{10,1... | collective-permute-start | bytes 1572872 | tf_op jit(solution)/shard_map/ppermute | solution.py:113
  665.3 0.8 copy-start.7
  666.1 12.9 %collective-permute-start.7 = (bf16[2,64,2048]{2,1,0:T(8,128)(2,1)S(1)}, bf16[2,64,2048]{2,1,0:T(8,128)(2,1)S(1)}, u32[]{:S(2)}, u32[]{:S(2)}) collective-permute-start(bf16[2,64,2048]{2,1,0:T(8,128)(2,1)S(1)} %collective-permute-done.6), channel_id=1, source_target_pairs={{0,1},{1,2},{2,3},{3,4},{4,5},{5,6},{6,7},{7,8},{8,9},{9,10},{10,1... | collective-permute-start | bytes 1572872 | tf_op jit(solution)/shard_map/ppermute | solution.py:113
  679.0 0.8 copy-start.9
  679.8 14.0 %collective-permute-start.8 = (bf16[2,64,2048]{2,1,0:T(8,128)(2,1)S(1)}, bf16[2,64,2048]{2,1,0:T(8,128)(2,1)S(1)}, u32[]{:S(2)}, u32[]{:S(2)}) collective-permute-start(bf16[2,64,2048]{2,1,0:T(8,128)(2,1)S(1)} %collective-permute-done.7), channel_id=1, source_target_pairs={{0,1},{1,2},{2,3},{3,4},{4,5},{5,6},{6,7},{7,8},{8,9},{9,10},{10,1... | collective-permute-start | bytes 1572872 | tf_op jit(solution)/shard_map/ppermute | solution.py:113
  693.8 0.8 copy-start.11
  694.6 15.1 %collective-permute-start.9 = (bf16[2,64,2048]{2,1,0:T(8,128)(2,1)S(1)}, bf16[2,64,2048]{2,1,0:T(8,128)(2,1)S(1)}, u32[]{:S(2)}, u32[]{:S(2)}) collective-permute-start(bf16[2,64,2048]{2,1,0:T(8,128)(2,1)S(1)} %collective-permute-done.8), channel_id=1, source_target_pairs={{0,1},{1,2},{2,3},{3,4},{4,5},{5,6},{6,7},{7,8},{8,9},{9,10},{10,1... | collective-permute-start | bytes 1572872 | tf_op jit(solution)/shard_map/ppermute | solution.py:113
  709.7 0.8 copy-start.13
  710.5 16.2 %collective-permute-start.10 = (bf16[2,64,2048]{2,1,0:T(8,128)(2,1)S(1)}, bf16[2,64,2048]{2,1,0:T(8,128)(2,1)S(1)}, u32[]{:S(2)}, u32[]{:S(2)}) collective-permute-start(bf16[2,64,2048]{2,1,0:T(8,128)(2,1)S(1)} %collective-permute-done.9), channel_id=1, source_target_pairs={{0,1},{1,2},{2,3},{3,4},{4,5},{5,6},{6,7},{7,8},{8,9},{9,10},{10,1... | collective-permute-start | bytes 1572872 | tf_op jit(solution)/shard_map/ppermute | solution.py:113
  726.7 0.8 copy-start.15
  727.5 17.3 %collective-permute-start.11 = (bf16[2,64,2048]{2,1,0:T(8,128)(2,1)S(1)}, bf16[2,64,2048]{2,1,0:T(8,128)(2,1)S(1)}, u32[]{:S(2)}, u32[]{:S(2)}) collective-permute-start(bf16[2,64,2048]{2,1,0:T(8,128)(2,1)S(1)} %collective-permute-done.10), channel_id=1, source_target_pairs={{0,1},{1,2},{2,3},{3,4},{4,5},{5,6},{6,7},{7,8},{8,9},{9,10},{10,1... | collective-permute-start | bytes 1572872 | tf_op jit(solution)/shard_map/ppermute | solution.py:113
  744.8 0.8 copy-start.17
  745.7 17.7 %collective-permute-start.12 = (bf16[2,64,2048]{2,1,0:T(8,128)(2,1)S(1)}, bf16[2,64,2048]{2,1,0:T(8,128)(2,1)S(1)}, u32[]{:S(2)}, u32[]{:S(2)}) collective-permute-start(bf16[2,64,2048]{2,1,0:T(8,128)(2,1)S(1)} %collective-permute-done.11), channel_id=1, source_target_pairs={{0,1},{1,2},{2,3},{3,4},{4,5},{5,6},{6,7},{7,8},{8,9},{9,10},{10,1... | collective-permute-start | bytes 1572872 | tf_op jit(solution)/shard_map/ppermute | solution.py:113
  763.4 0.8 copy-start.19
  764.2 16.5 %collective-permute-start.13 = (bf16[2,64,2048]{2,1,0:T(8,128)(2,1)S(1)}, bf16[2,64,2048]{2,1,0:T(8,128)(2,1)}, u32[]{:S(2)}, u32[]{:S(2)}) collective-permute-start(bf16[2,64,2048]{2,1,0:T(8,128)(2,1)S(1)} %collective-permute-done.12), channel_id=1, source_target_pairs={{0,1},{1,2},{2,3},{3,4},{4,5},{5,6},{6,7},{7,8},{8,9},{9,10},{10,1... | collective-permute-start | bytes 1572872 | tf_op jit(solution)/shard_map/ppermute | solution.py:113
  780.7 12.8 %collective-permute-start.14 = (bf16[2,64,2048]{2,1,0:T(8,128)(2,1)}, bf16[2,64,2048]{2,1,0:T(8,128)(2,1)}, u32[]{:S(2)}, u32[]{:S(2)}) collective-permute-start(bf16[2,64,2048]{2,1,0:T(8,128)(2,1)} %collective-permute-done.13), channel_id=1, source_target_pairs={{0,1},{1,2},{2,3},{3,4},{4,5},{5,6},{6,7},{7,8},{8,9},{9,10},{10,1... | collective-permute-start | bytes 1572872 | tf_op jit(solution)/shard_map/ppermute | solution.py:113
  780.7 16.6 %copy-start.20 = (bf16[2,64,2048]{2,1,0:T(8,128)(2,1)S(1)}, bf16[2,64,2048]{2,1,0:T(8,128)(2,1)}, u32[]{:S(2)}) copy-start(bf16[2,64,2048]{2,1,0:T(8,128)(2,1)} %copy-done.19) | copy-start | bytes 1572868
  780.7 17.4 %copy-start.18 = (bf16[2,64,2048]{2,1,0:T(8,128)(2,1)S(1)}, bf16[2,64,2048]{2,1,0:T(8,128)(2,1)}, u32[]{:S(2)}) copy-start(bf16[2,64,2048]{2,1,0:T(8,128)(2,1)} %copy-done.17) | copy-start | bytes 1572868
  780.7 18.3 %copy-start.16 = (bf16[2,64,2048]{2,1,0:T(8,128)(2,1)S(1)}, bf16[2,64,2048]{2,1,0:T(8,128)(2,1)}, u32[]{:S(2)}) copy-start(bf16[2,64,2048]{2,1,0:T(8,128)(2,1)} %copy-done.15) | copy-start | bytes 1572868
  780.7 19.1 %copy-start.14 = (bf16[2,64,2048]{2,1,0:T(8,128)(2,1)S(1)}, bf16[2,64,2048]{2,1,0:T(8,128)(2,1)}, u32[]{:S(2)}) copy-start(bf16[2,64,2048]{2,1,0:T(8,128)(2,1)} %copy-done.13) | copy-start | bytes 1572868
  780.8 19.9 %copy-start.12 = (bf16[2,64,2048]{2,1,0:T(8,128)(2,1)S(1)}, bf16[2,64,2048]{2,1,0:T(8,128)(2,1)}, u32[]{:S(2)}) copy-start(bf16[2,64,2048]{2,1,0:T(8,128)(2,1)} %copy-done.11) | copy-start | bytes 1572868
  780.8 20.8 %copy-start.10 = (bf16[2,64,2048]{2,1,0:T(8,128)(2,1)S(1)}, bf16[2,64,2048]{2,1,0:T(8,128)(2,1)}, u32[]{:S(2)}) copy-start(bf16[2,64,2048]{2,1,0:T(8,128)(2,1)} %copy-done.9) | copy-start | bytes 1572868
  780.8 21.6 %copy-start.8 = (bf16[2,64,2048]{2,1,0:T(8,128)(2,1)S(1)}, bf16[2,64,2048]{2,1,0:T(8,128)(2,1)}, u32[]{:S(2)}) copy-start(bf16[2,64,2048]{2,1,0:T(8,128)(2,1)} %copy-done.7) | copy-start | bytes 1572868
  780.8 22.4 %copy-start.6 = (bf16[2,64,2048]{2,1,0:T(8,128)(2,1)S(1)}, bf16[2,64,2048]{2,1,0:T(8,128)(2,1)}, u32[]{:S(2)}) copy-start(bf16[2,64,2048]{2,1,0:T(8,128)(2,1)} %copy-done.5) | copy-start | bytes 1572868
  832.9 8.5 copy-start.2
  841.4 13.2 %copy-start.4 = (bf16[1,1024,2048]{2,1,0:T(8,128)(2,1)S(1)}, bf16[1,1024,2048]{2,1,0:T(8,128)(2,1)}, u32[]{:S(2)}) copy-start(bf16[1,1024,2048]{2,1,0:T(8,128)(2,1)} %get-tuple-element.6) | copy-start | bytes 12582916
  841.4 13.2 %copy-start.22 = (bf16[1,1024,1024]{2,1,0:T(8,128)(2,1)S(1)}, bf16[1,1024,1024]{2,1,0:T(8,128)(2,1)}, u32[]{:S(2)}) copy-start(bf16[1,1024,1024]{2,1,0:T(8,128)(2,1)} %get-tuple-element.8) | copy-start | bytes 6291460
  854.6 6.9 copy-start.21
  861.5 10.8 %copy-start.3 = (f32[1,2048,1024]{2,1,0:T(8,128)S(1)}, f32[1,2048,1024]{2,1,0:T(8,128)}, u32[]{:S(2)}) copy-start(f32[1,2048,1024]{2,1,0:T(8,128)} %convolution_bitcast_fusion) | copy-start | bytes 25165828
  872.2 6.3 copy-start.1
Sparse Core Ops, SparseCore 0:
  577.0 33.3 all-gather.1
